TPU v7x, 32 devices: a whole 2x2x4 slice. The times are simulated.
32 devices in a mesh: segment: 2 (over x), slab: 16 (over z, y, core).
Axes of the slice: x: 2, y: 2, z: 4, core: 2. Of those that a mesh axis runs over, the one named last changes fastest.
Arguments:
- activations: bfloat16 [2, 2, 64, 8, 8, 128], P('segment', None, 'slab'), may hold values from -6 to 6
- weights: bfloat16 [2, 3456, 128], P('segment'), may hold values from -0.109375 to 0.109375
- out_grad: bfloat16 [2, 64, 8, 8, 128], P(None, 'slab'), may hold values from -6 to 6
Outputs:
- update: float32 [2, 3456, 128], P('segment')
- input_grads: bfloat16 [2, 2, 64, 8, 8, 128], P('segment', None, 'slab')
All inputs are finite; a program needn't handle non-finite values.
Results may differ from a plain program's by a relative error of at most 0.017.
Values may be sent and summed in bfloat16 or wider, within the bound.
No kernel may reach another device: no remote copies, remote signals or barrier semaphores. Data moves between devices by JAX's collectives and lax.ppermute only.
A program may use at most 64 MiB of HBM per device.

v0:
```python
import math
import jax
import jax.numpy as jnp
from jax import lax
from jax.sharding import PartitionSpec as P


def padded(cells, sides, width):
    for axis, dim in sides:
        count = lax.axis_size(axis)
        ends = count - 1
        head = lax.slice_in_dim(cells, 0, width, axis=dim)
        tail = lax.slice_in_dim(cells, cells.shape[dim] - width, cells.shape[dim], axis=dim)
        cells = jnp.concatenate(
            [
                lax.ppermute(tail, axis, [(i, (i + 1) % count) for i in range(ends)]),
                cells,
                lax.ppermute(head, axis, [((i + 1) % count, i) for i in range(ends)]),
            ],
            axis=dim,
        )
    return cells


def from_behind(block, axis, distance):
    devices = range(lax.axis_size(axis))
    route = [(i - distance, i) for i in devices if i - distance in devices]
    return lax.ppermute(block, axis, route)


def patches_of(rimmed):
    depth_count = rimmed.shape[0] - 2
    width_count = rimmed.shape[1]
    height = rimmed.shape[2]
    padded_all = jnp.pad(rimmed, ((0, 0), (1, 1), (1, 1), (0, 0)))
    pieces = []
    for offset in range(27):
        depth_off = offset // 9
        width_off = offset // 3 % 3
        height_off = offset % 3
        pieces.append(
            padded_all[
                depth_off : depth_off + depth_count,
                width_off : width_off + width_count,
                height_off : height_off + height,
            ]
        )
    joined = jnp.concatenate(pieces, axis=-1)
    return joined.reshape(depth_count * width_count * height, joined.shape[-1])


def shards(activations, weights, out_grad):
    stored_inputs = activations[0]
    weight = weights[0]
    channels = weight.shape[1]
    micro_count, depth_count, width_count, height = stored_inputs.shape[:4]
    cell_count = depth_count * width_count * height
    segments = lax.axis_size("segment")
    sindex = lax.axis_index("segment")
    flipped = (
        weight.reshape(27, channels, channels)[::-1]
        .transpose(0, 2, 1)
        .reshape(27 * channels, channels)
    )

    def advance(counter, state_tuple):
        incoming, partial_value, gradients = state_tuple
        micro_index = counter - (segments - 1 - sindex)
        active = (micro_index >= 0) & (micro_index < micro_count)
        chosen = jnp.clip(micro_index, 0, micro_count - 1)
        one_input = lax.dynamic_index_in_dim(stored_inputs, chosen, 0, False)
        rimmed_one = padded(one_input, (("slab", 0),), 1)
        patches = patches_of(rimmed_one)
        preact = jnp.dot(patches, weight, preferred_element_type=jnp.float32)
        from_loss = lax.dynamic_index_in_dim(out_grad, chosen, 0, False)
        upstream = (
            jnp.where(sindex == segments - 1, from_loss, incoming)
            .astype(jnp.float32)
            .reshape(cell_count, channels)
        )
        sigval = jax.nn.sigmoid(preact)
        deltas = jnp.where(active, upstream * sigval * (1.0 + preact * (1.0 - sigval)), 0.0).astype(
            jnp.bfloat16
        )
        partial_value = partial_value + lax.dot_general(
            patches, deltas, (((0,), (0,)), ((), ())), preferred_element_type=jnp.float32
        )
        delta_rim = padded(
            deltas.reshape(depth_count, width_count, height, channels), (("slab", 0),), 1
        )
        backward = jnp.dot(patches_of(delta_rim), flipped, preferred_element_type=jnp.float32)
        result = (
            (upstream + backward)
            .astype(jnp.bfloat16)
            .reshape(depth_count, width_count, height, channels)
        )
        current = lax.dynamic_index_in_dim(gradients, chosen, 0, False)
        gradients = lax.dynamic_update_index_in_dim(
            gradients, jnp.where(active, result, current), chosen, 0
        )
        incoming = from_behind(result, "segment", -1)
        return (incoming, partial_value, gradients)

    start_state = (
        jnp.zeros((depth_count, width_count, height, channels), jnp.bfloat16),
        jnp.zeros((27 * channels, channels), jnp.float32),
        jnp.zeros(stored_inputs.shape, jnp.bfloat16),
    )
    final_state = lax.fori_loop(0, segments + micro_count - 1, advance, start_state)
    partial_value = final_state[1]
    gradients = final_state[2]
    bound_value = math.sqrt(27.0 * channels * channels * segments)
    summed = lax.psum(partial_value, "slab")
    squares = lax.psum(jnp.sum(summed * summed), "segment")
    factor = jnp.minimum(1.0, bound_value / (jnp.sqrt(squares) + 1e-06))
    update = summed * factor
    return (update[None], gradients[None])


def solution(mesh):
    return jax.shard_map(
        shards,
        mesh=mesh,
        in_specs=(
            P("segment", None, "slab", None, None, None),
            P("segment", None, None),
            P(None, "slab", None, None, None),
        ),
        out_specs=(P("segment", None, None), P("segment", None, "slab", None, None, None)),
        check_vma=False,
    )
```

profile of v0, /device:TPU:0, one launch (start us, length us, event | category | flops | bytes accessed | tf_op | source)
XLA Modules:
  0.0 205.5 jit_solution(9570711436723103198)
XLA Ops:
  7.2 2.3 %copy.5 = bf16[27,128,128]{1,2,0:T(8,128)(2,1)} copy(bf16[27,128,128]{2,1,0:T(8,128)(2,1)} %bitcast.282) | data formatting | bytes 1769472 | tf_op jit(solution)/shard_map/reshape;squeeze | solution.py:61
  9.5 1.2 rev.3
  10.8 71.9 %while.20 = (s32[]{:T(128)}, bf16[4,8,8,128]{3,2,1,0:T(8,128)(2,1)S(1)}, f32[3456,128]{1,0:T(8,128)S(1)}, bf16[2,4,8,8,128]{4,3,2,1,0:T(8,128)(2,1)S(1)}, pred[]...) while((s32[]{:T(128)}, ...), condition=%wide.region_1.2_spmd.clone, body=%wide.region_0.1_spmd.clone.sunk | while | flops 684656640 | bytes 30519764 | solution.py:109
  10.9 1.3 collective-permute-start
  12.2 3.0 %collective-permute-start.1 = (bf16[1,8,8,128]{3,2,1,0:T(8,128)(2,1)S(1)}, bf16[1,8,8,128]{3,2,1,0:T(8,128)(2,1)S(1)}, u32[]{:S(2)}, u32[]{:S(2)}) collective-permute-start(bf16[1,8,8,128]{3,2,1,0:T(8,128)(2,1)S(1)} %get-tuple-element.463), channel_id=1, source_target_pairs={{0,1},{1,2},{2,3},{3,4},{4,5},{5,6},{6,7},{7,8},{8,9},{9,10},{10,1... | collective-permute-start | bytes 49160 | tf_op jit(solution)/shard_map/while/body/eval_jaxpr/ppermute | solution.py:16
  15.3 0.7 collective-permute-done.1
  18.3 1.3 collective-permute-start.2
  19.6 5.1 %collective-permute-start.3 = (bf16[1,8,8,128]{3,2,1,0:T(8,128)(2,1)S(1)}, bf16[1,8,8,128]{3,2,1,0:T(8,128)(2,1)S(1)}, u32[]{:S(2)}, u32[]{:S(2)}) collective-permute-start(bf16[1,8,8,128]{3,2,1,0:T(8,128)(2,1)S(1)} %get-tuple-element.492), channel_id=1, source_target_pairs={{0,1},{1,2},{2,3},{3,4},{4,5},{5,6},{6,7},{7,8},{8,9},{9,10},{10,1... | collective-permute-start | bytes 49160 | tf_op jit(solution)/shard_map/while/body/eval_jaxpr/ppermute | solution.py:16
  24.8 1.2 convolution_add_fusion.3
  27.7 1.3 collective-permute-start.4
  29.1 4.8 %collective-permute-done.4 = bf16[4,8,8,128]{3,2,1,0:T(8,128)(2,1)S(1)} collective-permute-done((bf16[4,8,8,128]{3,2,1,0:T(8,128)(2,1)S(1)}, bf16[4,8,8,128]{3,2,1,0:T(8,128)(2,1)S(1)}, u32[]{:S(2)}, u32[]{:S(2)}) %collective-permute-start.4) | collective-permute-done | bytes 65568 | tf_op jit(solution)/shard_map/while/body/eval_jaxpr/ppermute | solution.py:28
  33.9 1.3 collective-permute-start
  35.2 3.7 %collective-permute-start.1 = (bf16[1,8,8,128]{3,2,1,0:T(8,128)(2,1)S(1)}, bf16[1,8,8,128]{3,2,1,0:T(8,128)(2,1)S(1)}, u32[]{:S(2)}, u32[]{:S(2)}) collective-permute-start(bf16[1,8,8,128]{3,2,1,0:T(8,128)(2,1)S(1)} %get-tuple-element.463), channel_id=1, source_target_pairs={{0,1},{1,2},{2,3},{3,4},{4,5},{5,6},{6,7},{7,8},{8,9},{9,10},{10,1... | collective-permute-start | bytes 49160 | tf_op jit(solution)/shard_map/while/body/eval_jaxpr/ppermute | solution.py:16
  39.0 0.7 collective-permute-done.1
  42.0 1.3 collective-permute-start.2
  43.3 6.1 %collective-permute-start.3 = (bf16[1,8,8,128]{3,2,1,0:T(8,128)(2,1)S(1)}, bf16[1,8,8,128]{3,2,1,0:T(8,128)(2,1)S(1)}, u32[]{:S(2)}, u32[]{:S(2)}) collective-permute-start(bf16[1,8,8,128]{3,2,1,0:T(8,128)(2,1)S(1)} %get-tuple-element.492), channel_id=1, source_target_pairs={{0,1},{1,2},{2,3},{3,4},{4,5},{5,6},{6,7},{7,8},{8,9},{9,10},{10,1... | collective-permute-start | bytes 49160 | tf_op jit(solution)/shard_map/while/body/eval_jaxpr/ppermute | solution.py:16
  49.4 1.2 convolution_add_fusion.3
  52.3 1.3 collective-permute-start.4
  53.7 4.8 %collective-permute-done.4 = bf16[4,8,8,128]{3,2,1,0:T(8,128)(2,1)S(1)} collective-permute-done((bf16[4,8,8,128]{3,2,1,0:T(8,128)(2,1)S(1)}, bf16[4,8,8,128]{3,2,1,0:T(8,128)(2,1)S(1)}, u32[]{:S(2)}, u32[]{:S(2)}) %collective-permute-start.4) | collective-permute-done | bytes 65568 | tf_op jit(solution)/shard_map/while/body/eval_jaxpr/ppermute | solution.py:28
  58.5 1.3 collective-permute-start
  59.8 3.7 %collective-permute-start.1 = (bf16[1,8,8,128]{3,2,1,0:T(8,128)(2,1)S(1)}, bf16[1,8,8,128]{3,2,1,0:T(8,128)(2,1)S(1)}, u32[]{:S(2)}, u32[]{:S(2)}) collective-permute-start(bf16[1,8,8,128]{3,2,1,0:T(8,128)(2,1)S(1)} %get-tuple-element.463), channel_id=1, source_target_pairs={{0,1},{1,2},{2,3},{3,4},{4,5},{5,6},{6,7},{7,8},{8,9},{9,10},{10,1... | collective-permute-start | bytes 49160 | tf_op jit(solution)/shard_map/while/body/eval_jaxpr/ppermute | solution.py:16
  63.6 0.7 collective-permute-done.1
  66.6 1.3 collective-permute-start.2
  67.9 5.7 %collective-permute-start.3 = (bf16[1,8,8,128]{3,2,1,0:T(8,128)(2,1)S(1)}, bf16[1,8,8,128]{3,2,1,0:T(8,128)(2,1)S(1)}, u32[]{:S(2)}, u32[]{:S(2)}) collective-permute-start(bf16[1,8,8,128]{3,2,1,0:T(8,128)(2,1)S(1)} %get-tuple-element.492), channel_id=1, source_target_pairs={{0,1},{1,2},{2,3},{3,4},{4,5},{5,6},{6,7},{7,8},{8,9},{9,10},{10,1... | collective-permute-start | bytes 49160 | tf_op jit(solution)/shard_map/while/body/eval_jaxpr/ppermute | solution.py:16
  73.6 1.2 convolution_add_fusion.3
  76.5 1.3 collective-permute-start.4
  77.9 4.8 %collective-permute-done.4 = bf16[4,8,8,128]{3,2,1,0:T(8,128)(2,1)S(1)} collective-permute-done((bf16[4,8,8,128]{3,2,1,0:T(8,128)(2,1)S(1)}, bf16[4,8,8,128]{3,2,1,0:T(8,128)(2,1)S(1)}, u32[]{:S(2)}, u32[]{:S(2)}) %collective-permute-start.4) | collective-permute-done | bytes 65568 | tf_op jit(solution)/shard_map/while/body/eval_jaxpr/ppermute | solution.py:28
  82.7 1.2 copy-done
  83.9 104.4 %all-reduce.4.cloned.1.call-done = f32[3456,128]{1,0:T(8,128)} async-done(((f32[3456,128]{1,0:T(8,128)}), f32[3456,128]{1,0:T(8,128)}) %all-reduce.4.cloned.1.call-update) | async-done | bytes 1769488 | tf_op jit(solution)/shard_map/psum | solution.py:113
  188.3 2.7 %multiply_reduce_fusion = f32[]{:T(128)} fusion(f32[3456,128]{1,0:T(8,128)} %all-reduce.4.cloned.1.call-done), kind=kLoop, calls=%fused_computation.95 | loop fusion | flops 884735 | bytes 1769476 | tf_op jit(solution)/shard_map/reduce_sum | solution.py:114
  191.0 5.6 %psum.15 = f32[]{:T(128)} all-reduce(f32[]{:T(128)} %multiply_reduce_fusion), channel_id=1, replica_groups=mesh['segment'=2,'slab'=16] {'segment'}, use_global_device_ids=true, to_apply=%region_4.5 | all-reduce | flops 1 | bytes 8 | tf_op jit(solution)/shard_map/psum | solution.py:114
  197.3 1.3 multiply_bitcast_fusion
  (239 shorter events, 11.3 us)
Async XLA Ops:
  7.2 181.2 %all-reduce.4.cloned.1.call-start = ((), (), s32[]{:S(2)}) async-start(), calls=%async_computation | async-start | bytes 3538944 | tf_op jit(solution)/shard_map/psum | solution.py:113
  7.2 3.6 %copy-start.2 = (bf16[1,2,4,8,8,128]{5,4,3,2,1,0:T(8,128)(2,1)S(1)}, bf16[1,2,4,8,8,128]{5,4,3,2,1,0:T(8,128)(2,1)}, u32[]{:S(2)}) copy-start(bf16[1,2,4,8,8,128]{5,4,3,2,1,0:T(8,128)(2,1)} %param.5) | copy-start | bytes 393220
  7.2 3.6 %copy-start.5 = (bf16[2,4,8,8,128]{4,3,2,1,0:T(8,128)(2,1)S(1)}, bf16[2,4,8,8,128]{4,3,2,1,0:T(8,128)(2,1)}, u32[]{:S(2)}) copy-start(bf16[2,4,8,8,128]{4,3,2,1,0:T(8,128)(2,1)} %param.7) | copy-start | bytes 393220
  10.9 4.4 %collective-permute-start = (bf16[1,8,8,128]{3,2,1,0:T(8,128)(2,1)S(1)}, bf16[1,8,8,128]{3,2,1,0:T(8,128)(2,1)S(1)}, u32[]{:S(2)}, u32[]{:S(2)}) collective-permute-start(bf16[1,8,8,128]{3,2,1,0:T(8,128)(2,1)S(1)} %get-tuple-element.462), channel_id=1, source_target_pairs={{1,0},{2,1},{3,2},{4,3},{5,4},{6,5},{7,6},{8,7},{9,8},{10,9},{11,1... | collective-permute-start | bytes 49160 | tf_op jit(solution)/shard_map/while/body/eval_jaxpr/ppermute | solution.py:18
  12.2 3.9 %collective-permute-start.1 = (bf16[1,8,8,128]{3,2,1,0:T(8,128)(2,1)S(1)}, bf16[1,8,8,128]{3,2,1,0:T(8,128)(2,1)S(1)}, u32[]{:S(2)}, u32[]{:S(2)}) collective-permute-start(bf16[1,8,8,128]{3,2,1,0:T(8,128)(2,1)S(1)} %get-tuple-element.463), channel_id=1, source_target_pairs={{0,1},{1,2},{2,3},{3,4},{4,5},{5,6},{6,7},{7,8},{8,9},{9,10},{10,1... | collective-permute-start | bytes 49160 | tf_op jit(solution)/shard_map/while/body/eval_jaxpr/ppermute | solution.py:16
  16.4 1.2 copy-start.4
  18.3 7.6 %collective-permute-start.2 = (bf16[1,8,8,128]{3,2,1,0:T(8,128)(2,1)S(1)}, bf16[1,8,8,128]{3,2,1,0:T(8,128)(2,1)S(1)}, u32[]{:S(2)}, u32[]{:S(2)}) collective-permute-start(bf16[1,8,8,128]{3,2,1,0:T(8,128)(2,1)S(1)} %get-tuple-element.491), channel_id=1, source_target_pairs={{1,0},{2,1},{3,2},{4,3},{5,4},{6,5},{7,6},{8,7},{9,8},{10,9},{11,1... | collective-permute-start | bytes 49160 | tf_op jit(solution)/shard_map/while/body/eval_jaxpr/ppermute | solution.py:18
  19.6 6.3 %collective-permute-start.3 = (bf16[1,8,8,128]{3,2,1,0:T(8,128)(2,1)S(1)}, bf16[1,8,8,128]{3,2,1,0:T(8,128)(2,1)S(1)}, u32[]{:S(2)}, u32[]{:S(2)}) collective-permute-start(bf16[1,8,8,128]{3,2,1,0:T(8,128)(2,1)S(1)} %get-tuple-element.492), channel_id=1, source_target_pairs={{0,1},{1,2},{2,3},{3,4},{4,5},{5,6},{6,7},{7,8},{8,9},{9,10},{10,1... | collective-permute-start | bytes 49160 | tf_op jit(solution)/shard_map/while/body/eval_jaxpr/ppermute | solution.py:16
  27.7 6.2 %collective-permute-start.4 = (bf16[4,8,8,128]{3,2,1,0:T(8,128)(2,1)S(1)}, bf16[4,8,8,128]{3,2,1,0:T(8,128)(2,1)S(1)}, u32[]{:S(2)}, u32[]{:S(2)}) collective-permute-start(bf16[4,8,8,128]{3,2,1,0:T(8,128)(2,1)S(1)} %bitcast.225), channel_id=1, source_target_pairs={{16,0},{17,1},{18,2},{19,3},{20,4},{21,5},{22,6},{23,7},{24,8},{25... | collective-permute-start | bytes 196616 | tf_op jit(solution)/shard_map/while/body/eval_jaxpr/ppermute | solution.py:28
  33.9 5.1 %collective-permute-start = (bf16[1,8,8,128]{3,2,1,0:T(8,128)(2,1)S(1)}, bf16[1,8,8,128]{3,2,1,0:T(8,128)(2,1)S(1)}, u32[]{:S(2)}, u32[]{:S(2)}) collective-permute-start(bf16[1,8,8,128]{3,2,1,0:T(8,128)(2,1)S(1)} %get-tuple-element.462), channel_id=1, source_target_pairs={{1,0},{2,1},{3,2},{4,3},{5,4},{6,5},{7,6},{8,7},{9,8},{10,9},{11,1... | collective-permute-start | bytes 49160 | tf_op jit(solution)/shard_map/while/body/eval_jaxpr/ppermute | solution.py:18
  35.2 4.5 %collective-permute-start.1 = (bf16[1,8,8,128]{3,2,1,0:T(8,128)(2,1)S(1)}, bf16[1,8,8,128]{3,2,1,0:T(8,128)(2,1)S(1)}, u32[]{:S(2)}, u32[]{:S(2)}) collective-permute-start(bf16[1,8,8,128]{3,2,1,0:T(8,128)(2,1)S(1)} %get-tuple-element.463), channel_id=1, source_target_pairs={{0,1},{1,2},{2,3},{3,4},{4,5},{5,6},{6,7},{7,8},{8,9},{9,10},{10,1... | collective-permute-start | bytes 49160 | tf_op jit(solution)/shard_map/while/body/eval_jaxpr/ppermute | solution.py:16
  40.1 1.2 copy-start.4
  42.0 8.6 %collective-permute-start.2 = (bf16[1,8,8,128]{3,2,1,0:T(8,128)(2,1)S(1)}, bf16[1,8,8,128]{3,2,1,0:T(8,128)(2,1)S(1)}, u32[]{:S(2)}, u32[]{:S(2)}) collective-permute-start(bf16[1,8,8,128]{3,2,1,0:T(8,128)(2,1)S(1)} %get-tuple-element.491), channel_id=1, source_target_pairs={{1,0},{2,1},{3,2},{4,3},{5,4},{6,5},{7,6},{8,7},{9,8},{10,9},{11,1... | collective-permute-start | bytes 49160 | tf_op jit(solution)/shard_map/while/body/eval_jaxpr/ppermute | solution.py:18
  43.3 7.3 %collective-permute-start.3 = (bf16[1,8,8,128]{3,2,1,0:T(8,128)(2,1)S(1)}, bf16[1,8,8,128]{3,2,1,0:T(8,128)(2,1)S(1)}, u32[]{:S(2)}, u32[]{:S(2)}) collective-permute-start(bf16[1,8,8,128]{3,2,1,0:T(8,128)(2,1)S(1)} %get-tuple-element.492), channel_id=1, source_target_pairs={{0,1},{1,2},{2,3},{3,4},{4,5},{5,6},{6,7},{7,8},{8,9},{9,10},{10,1... | collective-permute-start | bytes 49160 | tf_op jit(solution)/shard_map/while/body/eval_jaxpr/ppermute | solution.py:16
  52.3 6.2 %collective-permute-start.4 = (bf16[4,8,8,128]{3,2,1,0:T(8,128)(2,1)S(1)}, bf16[4,8,8,128]{3,2,1,0:T(8,128)(2,1)S(1)}, u32[]{:S(2)}, u32[]{:S(2)}) collective-permute-start(bf16[4,8,8,128]{3,2,1,0:T(8,128)(2,1)S(1)} %bitcast.225), channel_id=1, source_target_pairs={{16,0},{17,1},{18,2},{19,3},{20,4},{21,5},{22,6},{23,7},{24,8},{25... | collective-permute-start | bytes 196616 | tf_op jit(solution)/shard_map/while/body/eval_jaxpr/ppermute | solution.py:28
  58.5 5.1 %collective-permute-start = (bf16[1,8,8,128]{3,2,1,0:T(8,128)(2,1)S(1)}, bf16[1,8,8,128]{3,2,1,0:T(8,128)(2,1)S(1)}, u32[]{:S(2)}, u32[]{:S(2)}) collective-permute-start(bf16[1,8,8,128]{3,2,1,0:T(8,128)(2,1)S(1)} %get-tuple-element.462), channel_id=1, source_target_pairs={{1,0},{2,1},{3,2},{4,3},{5,4},{6,5},{7,6},{8,7},{9,8},{10,9},{11,1... | collective-permute-start | bytes 49160 | tf_op jit(solution)/shard_map/while/body/eval_jaxpr/ppermute | solution.py:18
  59.8 4.5 %collective-permute-start.1 = (bf16[1,8,8,128]{3,2,1,0:T(8,128)(2,1)S(1)}, bf16[1,8,8,128]{3,2,1,0:T(8,128)(2,1)S(1)}, u32[]{:S(2)}, u32[]{:S(2)}) collective-permute-start(bf16[1,8,8,128]{3,2,1,0:T(8,128)(2,1)S(1)} %get-tuple-element.463), channel_id=1, source_target_pairs={{0,1},{1,2},{2,3},{3,4},{4,5},{5,6},{6,7},{7,8},{8,9},{9,10},{10,1... | collective-permute-start | bytes 49160 | tf_op jit(solution)/shard_map/while/body/eval_jaxpr/ppermute | solution.py:16
  64.7 1.2 copy-start.4
  66.6 8.1 %collective-permute-start.2 = (bf16[1,8,8,128]{3,2,1,0:T(8,128)(2,1)S(1)}, bf16[1,8,8,128]{3,2,1,0:T(8,128)(2,1)S(1)}, u32[]{:S(2)}, u32[]{:S(2)}) collective-permute-start(bf16[1,8,8,128]{3,2,1,0:T(8,128)(2,1)S(1)} %get-tuple-element.491), channel_id=1, source_target_pairs={{1,0},{2,1},{3,2},{4,3},{5,4},{6,5},{7,6},{8,7},{9,8},{10,9},{11,1... | collective-permute-start | bytes 49160 | tf_op jit(solution)/shard_map/while/body/eval_jaxpr/ppermute | solution.py:18
  67.9 6.9 %collective-permute-start.3 = (bf16[1,8,8,128]{3,2,1,0:T(8,128)(2,1)S(1)}, bf16[1,8,8,128]{3,2,1,0:T(8,128)(2,1)S(1)}, u32[]{:S(2)}, u32[]{:S(2)}) collective-permute-start(bf16[1,8,8,128]{3,2,1,0:T(8,128)(2,1)S(1)} %get-tuple-element.492), channel_id=1, source_target_pairs={{0,1},{1,2},{2,3},{3,4},{4,5},{5,6},{6,7},{7,8},{8,9},{9,10},{10,1... | collective-permute-start | bytes 49160 | tf_op jit(solution)/shard_map/while/body/eval_jaxpr/ppermute | solution.py:16
  76.5 6.2 %collective-permute-start.4 = (bf16[4,8,8,128]{3,2,1,0:T(8,128)(2,1)S(1)}, bf16[4,8,8,128]{3,2,1,0:T(8,128)(2,1)S(1)}, u32[]{:S(2)}, u32[]{:S(2)}) collective-permute-start(bf16[4,8,8,128]{3,2,1,0:T(8,128)(2,1)S(1)} %bitcast.225), channel_id=1, source_target_pairs={{16,0},{17,1},{18,2},{19,3},{20,4},{21,5},{22,6},{23,7},{24,8},{25... | collective-permute-start | bytes 196616 | tf_op jit(solution)/shard_map/while/body/eval_jaxpr/ppermute | solution.py:28
  82.7 1.2 copy-start
  82.7 108.3 %copy-start.3 = (bf16[2,4,8,8,128]{4,3,2,1,0:T(8,128)(2,1)}, bf16[2,4,8,8,128]{4,3,2,1,0:T(8,128)(2,1)S(1)}, u32[]{:S(2)}) copy-start(bf16[2,4,8,8,128]{4,3,2,1,0:T(8,128)(2,1)S(1)} %get-tuple-element.231) | copy-start | bytes 393220
  188.3 9.0 %copy-start.1 = (f32[3456,128]{1,0:T(8,128)S(1)}, f32[3456,128]{1,0:T(8,128)}, u32[]{:S(2)}) copy-start(f32[3456,128]{1,0:T(8,128)} %all-reduce.4.cloned.1.call-done) | copy-start | bytes 5308420
Sparse Core Ops, SparseCore 0:
  84.0 104.2 all-reduce.3
where the time goes:
time: 206 us; the launch traced here: 205 us
  waiting for transfers between devices  121 us (59%)
  starting transfers between devices  38.9 us (19%)
  between operations  14.8 us (7%)
  local copies, waits for them, and re-layouts  11 us (5%)
  matrix products  7.38 us (4%)
  blocking collectives  5.55 us (3%)
  other arithmetic  5.06 us (2%)
    psum x1, waiting for transfers between devices, shards(): summed = lax.psum(partial_value, 'slab')  104 us
    ppermute x6, starting transfers between devices, padded(): lax.ppermute(tail, axis, [(i, (i + 1) % count) for i in range(ends)])  27.3 us
    ppermute x3, waiting for transfers between devices, from_behind(): return lax.ppermute(block, axis, route)  14.5 us
    ppermute x6, starting transfers between devices, padded(): lax.ppermute(head, axis, [((i + 1) % count, i) for i in range(ends)])  7.73 us
    psum x1, blocking collectives, shards(): squares = lax.psum(jnp.sum(summed * summed), 'segment')  5.55 us
    while x159, local copies, waits for them, and re-layouts  4.43 us
  transfers between devices with their start and end apart: 16, of which 7 were waited for; matrix products, arithmetic and copies ran while one was open for 2% of the time, Pallas kernels for 0%

commit v1 on v0

--- a/solution.py
+++ b/solution.py
@@ -110,7 +110,8 @@
     partial_value = final_state[1]
     gradients = final_state[2]
     bound_value = math.sqrt(27.0 * channels * channels * segments)
-    summed = lax.psum(partial_value, "slab")
+    parts = lax.all_gather(partial_value, "slab", axis=0, tiled=False)
+    summed = parts.sum(axis=0)
     squares = lax.psum(jnp.sum(summed * summed), "segment")
     factor = jnp.minimum(1.0, bound_value / (jnp.sqrt(squares) + 1e-06))
     update = summed * factor

time: 206 us -> 262 us (1.27)
  waiting for transfers between devices: 121 us -> 168 us
  other arithmetic: 5.06 us -> 14.2 us
    all_gather x0 -> x1, waiting for transfers between devices: none -> 151 us  [shards(): parts = lax.all_gather(partial_value, 'slab', axis=0, tiled=False)]
    psum x1 -> x0, waiting for transfers between devices: 104 us -> none  [shards(): summed = lax.psum(partial_value, 'slab')]
    reduce_sum x0 -> x1, other arithmetic: none -> 10.7 us  [shards(): summed = parts.sum(axis=0)]
  transfers between devices with their start and end apart: 16 -> 16, of which waited for: 7 -> 7; matrix products, arithmetic and copies ran while one was open for 2% -> 1% of each run, Pallas kernels for 0% -> 0%
where the time goes in v1:
time: 262 us; the launch traced here: 261 us
  waiting for transfers between devices  168 us (64%)
  starting transfers between devices  38.9 us (15%)
  between operations  14.8 us (6%)
  other arithmetic  14.2 us (5%)
  local copies, waits for them, and re-layouts  11 us (4%)
  matrix products  7.39 us (3%)
  blocking collectives  5.55 us (2%)
    all_gather x1, waiting for transfers between devices, shards(): parts = lax.all_gather(partial_value, 'slab', axis=0, tiled=False)  151 us
    ppermute x6, starting transfers between devices, padded(): lax.ppermute(tail, axis, [(i, (i + 1) % count) for i in range(ends)])  27.3 us
    ppermute x3, waiting for transfers between devices, from_behind(): return lax.ppermute(block, axis, route)  14.5 us
    reduce_sum x1, other arithmetic, shards(): summed = parts.sum(axis=0)  10.7 us
    ppermute x6, starting transfers between devices, padded(): lax.ppermute(head, axis, [((i + 1) % count, i) for i in range(ends)])  7.73 us
    psum x1, blocking collectives, shards(): squares = lax.psum(jnp.sum(summed * summed), 'segment')  5.55 us
  transfers between devices with their start and end apart: 16, of which 7 were waited for; matrix products, arithmetic and copies ran while one was open for 1% of the time, Pallas kernels for 0%

profile of v1, /device:TPU:0, one launch (start us, length us, event | category | flops | bytes accessed | tf_op | source)
XLA Modules:
  0.0 261.5 jit_solution(8642884717805192174)
XLA Ops:
  7.2 2.3 copy.5
  9.5 1.2 rev.3
  10.8 71.9 %while.20 = (s32[]{:T(128)}, bf16[4,8,8,128]{3,2,1,0:T(8,128)(2,1)S(1)}, f32[3456,128]{1,0:T(8,128)S(1)}, bf16[2,4,8,8,128]{4,3,2,1,0:T(8,128)(2,1)S(1)}, pred[]...) while((s32[]{:T(128)}, ...), condition=%wide.region_1.2_spmd.clone, body=%wide.region_0.1_spmd.clone.sunk | while | flops 684656640 | bytes 30519772 | solution.py:109
  10.8 1.3 collective-permute-start
  12.1 3.0 %collective-permute-start.1 = (bf16[1,8,8,128]{3,2,1,0:T(8,128)(2,1)S(1)}, bf16[1,8,8,128]{3,2,1,0:T(8,128)(2,1)S(1)}, u32[]{:S(2)}, u32[]{:S(2)}) collective-permute-start(bf16[1,8,8,128]{3,2,1,0:T(8,128)(2,1)S(1)} %get-tuple-element.463), channel_id=1, source_target_pairs={{0,1},{1,2},{2,3},{3,4},{4,5},{5,6},{6,7},{7,8},{8,9},{9,10},{10,1... | collective-permute-start | bytes 49160 | tf_op jit(solution)/shard_map/while/body/eval_jaxpr/ppermute | solution.py:16
  15.3 0.7 collective-permute-done.1
  18.3 1.3 collective-permute-start.2
  19.6 5.1 %collective-permute-start.3 = (bf16[1,8,8,128]{3,2,1,0:T(8,128)(2,1)S(1)}, bf16[1,8,8,128]{3,2,1,0:T(8,128)(2,1)S(1)}, u32[]{:S(2)}, u32[]{:S(2)}) collective-permute-start(bf16[1,8,8,128]{3,2,1,0:T(8,128)(2,1)S(1)} %get-tuple-element.492), channel_id=1, source_target_pairs={{0,1},{1,2},{2,3},{3,4},{4,5},{5,6},{6,7},{7,8},{8,9},{9,10},{10,1... | collective-permute-start | bytes 49160 | tf_op jit(solution)/shard_map/while/body/eval_jaxpr/ppermute | solution.py:16
  24.7 1.2 convolution_add_fusion.3
  27.7 1.3 collective-permute-start.4
  29.1 4.8 %collective-permute-done.4 = bf16[4,8,8,128]{3,2,1,0:T(8,128)(2,1)S(1)} collective-permute-done((bf16[4,8,8,128]{3,2,1,0:T(8,128)(2,1)S(1)}, bf16[4,8,8,128]{3,2,1,0:T(8,128)(2,1)S(1)}, u32[]{:S(2)}, u32[]{:S(2)}) %collective-permute-start.4) | collective-permute-done | bytes 65568 | tf_op jit(solution)/shard_map/while/body/eval_jaxpr/ppermute | solution.py:28
  33.9 1.3 collective-permute-start
  35.2 3.7 %collective-permute-start.1 = (bf16[1,8,8,128]{3,2,1,0:T(8,128)(2,1)S(1)}, bf16[1,8,8,128]{3,2,1,0:T(8,128)(2,1)S(1)}, u32[]{:S(2)}, u32[]{:S(2)}) collective-permute-start(bf16[1,8,8,128]{3,2,1,0:T(8,128)(2,1)S(1)} %get-tuple-element.463), channel_id=1, source_target_pairs={{0,1},{1,2},{2,3},{3,4},{4,5},{5,6},{6,7},{7,8},{8,9},{9,10},{10,1... | collective-permute-start | bytes 49160 | tf_op jit(solution)/shard_map/while/body/eval_jaxpr/ppermute | solution.py:16
  39.0 0.7 collective-permute-done.1
  42.0 1.3 collective-permute-start.2
  43.3 6.1 %collective-permute-start.3 = (bf16[1,8,8,128]{3,2,1,0:T(8,128)(2,1)S(1)}, bf16[1,8,8,128]{3,2,1,0:T(8,128)(2,1)S(1)}, u32[]{:S(2)}, u32[]{:S(2)}) collective-permute-start(bf16[1,8,8,128]{3,2,1,0:T(8,128)(2,1)S(1)} %get-tuple-element.492), channel_id=1, source_target_pairs={{0,1},{1,2},{2,3},{3,4},{4,5},{5,6},{6,7},{7,8},{8,9},{9,10},{10,1... | collective-permute-start | bytes 49160 | tf_op jit(solution)/shard_map/while/body/eval_jaxpr/ppermute | solution.py:16
  49.4 1.2 convolution_add_fusion.3
  52.4 1.3 collective-permute-start.4
  53.7 4.8 %collective-permute-done.4 = bf16[4,8,8,128]{3,2,1,0:T(8,128)(2,1)S(1)} collective-permute-done((bf16[4,8,8,128]{3,2,1,0:T(8,128)(2,1)S(1)}, bf16[4,8,8,128]{3,2,1,0:T(8,128)(2,1)S(1)}, u32[]{:S(2)}, u32[]{:S(2)}) %collective-permute-start.4) | collective-permute-done | bytes 65568 | tf_op jit(solution)/shard_map/while/body/eval_jaxpr/ppermute | solution.py:28
  58.5 1.3 collective-permute-start
  59.8 3.7 %collective-permute-start.1 = (bf16[1,8,8,128]{3,2,1,0:T(8,128)(2,1)S(1)}, bf16[1,8,8,128]{3,2,1,0:T(8,128)(2,1)S(1)}, u32[]{:S(2)}, u32[]{:S(2)}) collective-permute-start(bf16[1,8,8,128]{3,2,1,0:T(8,128)(2,1)S(1)} %get-tuple-element.463), channel_id=1, source_target_pairs={{0,1},{1,2},{2,3},{3,4},{4,5},{5,6},{6,7},{7,8},{8,9},{9,10},{10,1... | collective-permute-start | bytes 49160 | tf_op jit(solution)/shard_map/while/body/eval_jaxpr/ppermute | solution.py:16
  66.6 1.3 collective-permute-start.2
  67.9 5.7 %collective-permute-start.3 = (bf16[1,8,8,128]{3,2,1,0:T(8,128)(2,1)S(1)}, bf16[1,8,8,128]{3,2,1,0:T(8,128)(2,1)S(1)}, u32[]{:S(2)}, u32[]{:S(2)}) collective-permute-start(bf16[1,8,8,128]{3,2,1,0:T(8,128)(2,1)S(1)} %get-tuple-element.492), channel_id=1, source_target_pairs={{0,1},{1,2},{2,3},{3,4},{4,5},{5,6},{6,7},{7,8},{8,9},{9,10},{10,1... | collective-permute-start | bytes 49160 | tf_op jit(solution)/shard_map/while/body/eval_jaxpr/ppermute | solution.py:16
  73.6 1.2 convolution_add_fusion.3
  76.6 1.3 collective-permute-start.4
  77.9 4.8 %collective-permute-done.4 = bf16[4,8,8,128]{3,2,1,0:T(8,128)(2,1)S(1)} collective-permute-done((bf16[4,8,8,128]{3,2,1,0:T(8,128)(2,1)S(1)}, bf16[4,8,8,128]{3,2,1,0:T(8,128)(2,1)S(1)}, u32[]{:S(2)}, u32[]{:S(2)}) %collective-permute-start.4) | collective-permute-done | bytes 65568 | tf_op jit(solution)/shard_map/while/body/eval_jaxpr/ppermute | solution.py:28
  82.7 1.2 copy-done
  84.0 151.3 %all-gather.3.cloned.1.call-done = f32[55296,128]{1,0:T(8,128)} async-done(((f32[3456,128]{1,0:T(8,128)}), f32[55296,128]{1,0:T(8,128)}) %all-gather.3.cloned.1.call-update) | async-done | bytes 28311568 | tf_op jit(solution)/shard_map/all_gather | solution.py:113
  235.2 10.7 %reduce_sum.18 = f32[3456,128]{1,0:T(8,128)S(1)} reduce(f32[16,3456,128]{2,1,0:T(8,128)} %bitcast.221, f32[]{:T(128)} %constant.83.clone.1), dimensions={0}, to_apply=%region_2.3 | reduce | flops 6635520 | bytes 30081028 | tf_op jit(solution)/shard_map/reduce_sum | solution.py:114
  246.0 1.1 multiply_reduce_fusion
  247.0 5.5 %psum.7 = f32[]{:T(128)} all-reduce(f32[]{:T(128)} %multiply_reduce_fusion), channel_id=1, replica_groups=mesh['segment'=2,'slab'=16] {'segment'}, use_global_device_ids=true, to_apply=%region_4.5 | all-reduce | flops 1 | bytes 8 | tf_op jit(solution)/shard_map/psum | solution.py:115
  253.3 1.3 multiply_bitcast_fusion
  (238 shorter events, 12.1 us)
Async XLA Ops:
  7.2 228.1 %all-gather.3.cloned.1.call-start = ((), (), s32[]{:S(2)}) async-start(), calls=%async_computation | async-start | bytes 30081024 | tf_op jit(solution)/shard_map/all_gather | solution.py:113
  7.2 3.6 %copy-start.1 = (bf16[1,2,4,8,8,128]{5,4,3,2,1,0:T(8,128)(2,1)S(1)}, bf16[1,2,4,8,8,128]{5,4,3,2,1,0:T(8,128)(2,1)}, u32[]{:S(2)}) copy-start(bf16[1,2,4,8,8,128]{5,4,3,2,1,0:T(8,128)(2,1)} %param.5) | copy-start | bytes 393220
  7.2 3.6 %copy-start.4 = (bf16[2,4,8,8,128]{4,3,2,1,0:T(8,128)(2,1)S(1)}, bf16[2,4,8,8,128]{4,3,2,1,0:T(8,128)(2,1)}, u32[]{:S(2)}) copy-start(bf16[2,4,8,8,128]{4,3,2,1,0:T(8,128)(2,1)} %param.7) | copy-start | bytes 393220
  10.8 4.4 %collective-permute-start = (bf16[1,8,8,128]{3,2,1,0:T(8,128)(2,1)S(1)}, bf16[1,8,8,128]{3,2,1,0:T(8,128)(2,1)S(1)}, u32[]{:S(2)}, u32[]{:S(2)}) collective-permute-start(bf16[1,8,8,128]{3,2,1,0:T(8,128)(2,1)S(1)} %get-tuple-element.462), channel_id=1, source_target_pairs={{1,0},{2,1},{3,2},{4,3},{5,4},{6,5},{7,6},{8,7},{9,8},{10,9},{11,1... | collective-permute-start | bytes 49160 | tf_op jit(solution)/shard_map/while/body/eval_jaxpr/ppermute | solution.py:18
  12.1 3.9 %collective-permute-start.1 = (bf16[1,8,8,128]{3,2,1,0:T(8,128)(2,1)S(1)}, bf16[1,8,8,128]{3,2,1,0:T(8,128)(2,1)S(1)}, u32[]{:S(2)}, u32[]{:S(2)}) collective-permute-start(bf16[1,8,8,128]{3,2,1,0:T(8,128)(2,1)S(1)} %get-tuple-element.463), channel_id=1, source_target_pairs={{0,1},{1,2},{2,3},{3,4},{4,5},{5,6},{6,7},{7,8},{8,9},{9,10},{10,1... | collective-permute-start | bytes 49160 | tf_op jit(solution)/shard_map/while/body/eval_jaxpr/ppermute | solution.py:16
  16.4 1.2 copy-start.3
  18.3 7.6 %collective-permute-start.2 = (bf16[1,8,8,128]{3,2,1,0:T(8,128)(2,1)S(1)}, bf16[1,8,8,128]{3,2,1,0:T(8,128)(2,1)S(1)}, u32[]{:S(2)}, u32[]{:S(2)}) collective-permute-start(bf16[1,8,8,128]{3,2,1,0:T(8,128)(2,1)S(1)} %get-tuple-element.491), channel_id=1, source_target_pairs={{1,0},{2,1},{3,2},{4,3},{5,4},{6,5},{7,6},{8,7},{9,8},{10,9},{11,1... | collective-permute-start | bytes 49160 | tf_op jit(solution)/shard_map/while/body/eval_jaxpr/ppermute | solution.py:18
  19.6 6.3 %collective-permute-start.3 = (bf16[1,8,8,128]{3,2,1,0:T(8,128)(2,1)S(1)}, bf16[1,8,8,128]{3,2,1,0:T(8,128)(2,1)S(1)}, u32[]{:S(2)}, u32[]{:S(2)}) collective-permute-start(bf16[1,8,8,128]{3,2,1,0:T(8,128)(2,1)S(1)} %get-tuple-element.492), channel_id=1, source_target_pairs={{0,1},{1,2},{2,3},{3,4},{4,5},{5,6},{6,7},{7,8},{8,9},{9,10},{10,1... | collective-permute-start | bytes 49160 | tf_op jit(solution)/shard_map/while/body/eval_jaxpr/ppermute | solution.py:16
  27.7 6.2 %collective-permute-start.4 = (bf16[4,8,8,128]{3,2,1,0:T(8,128)(2,1)S(1)}, bf16[4,8,8,128]{3,2,1,0:T(8,128)(2,1)S(1)}, u32[]{:S(2)}, u32[]{:S(2)}) collective-permute-start(bf16[4,8,8,128]{3,2,1,0:T(8,128)(2,1)S(1)} %bitcast.227), channel_id=1, source_target_pairs={{16,0},{17,1},{18,2},{19,3},{20,4},{21,5},{22,6},{23,7},{24,8},{25... | collective-permute-start | bytes 196616 | tf_op jit(solution)/shard_map/while/body/eval_jaxpr/ppermute | solution.py:28
  33.9 5.1 %collective-permute-start = (bf16[1,8,8,128]{3,2,1,0:T(8,128)(2,1)S(1)}, bf16[1,8,8,128]{3,2,1,0:T(8,128)(2,1)S(1)}, u32[]{:S(2)}, u32[]{:S(2)}) collective-permute-start(bf16[1,8,8,128]{3,2,1,0:T(8,128)(2,1)S(1)} %get-tuple-element.462), channel_id=1, source_target_pairs={{1,0},{2,1},{3,2},{4,3},{5,4},{6,5},{7,6},{8,7},{9,8},{10,9},{11,1... | collective-permute-start | bytes 49160 | tf_op jit(solution)/shard_map/while/body/eval_jaxpr/ppermute | solution.py:18
  35.2 4.5 %collective-permute-start.1 = (bf16[1,8,8,128]{3,2,1,0:T(8,128)(2,1)S(1)}, bf16[1,8,8,128]{3,2,1,0:T(8,128)(2,1)S(1)}, u32[]{:S(2)}, u32[]{:S(2)}) collective-permute-start(bf16[1,8,8,128]{3,2,1,0:T(8,128)(2,1)S(1)} %get-tuple-element.463), channel_id=1, source_target_pairs={{0,1},{1,2},{2,3},{3,4},{4,5},{5,6},{6,7},{7,8},{8,9},{9,10},{10,1... | collective-permute-start | bytes 49160 | tf_op jit(solution)/shard_map/while/body/eval_jaxpr/ppermute | solution.py:16
  40.1 1.2 copy-start.3
  42.0 8.6 %collective-permute-start.2 = (bf16[1,8,8,128]{3,2,1,0:T(8,128)(2,1)S(1)}, bf16[1,8,8,128]{3,2,1,0:T(8,128)(2,1)S(1)}, u32[]{:S(2)}, u32[]{:S(2)}) collective-permute-start(bf16[1,8,8,128]{3,2,1,0:T(8,128)(2,1)S(1)} %get-tuple-element.491), channel_id=1, source_target_pairs={{1,0},{2,1},{3,2},{4,3},{5,4},{6,5},{7,6},{8,7},{9,8},{10,9},{11,1... | collective-permute-start | bytes 49160 | tf_op jit(solution)/shard_map/while/body/eval_jaxpr/ppermute | solution.py:18
  43.3 7.3 %collective-permute-start.3 = (bf16[1,8,8,128]{3,2,1,0:T(8,128)(2,1)S(1)}, bf16[1,8,8,128]{3,2,1,0:T(8,128)(2,1)S(1)}, u32[]{:S(2)}, u32[]{:S(2)}) collective-permute-start(bf16[1,8,8,128]{3,2,1,0:T(8,128)(2,1)S(1)} %get-tuple-element.492), channel_id=1, source_target_pairs={{0,1},{1,2},{2,3},{3,4},{4,5},{5,6},{6,7},{7,8},{8,9},{9,10},{10,1... | collective-permute-start | bytes 49160 | tf_op jit(solution)/shard_map/while/body/eval_jaxpr/ppermute | solution.py:16
  52.4 6.2 %collective-permute-start.4 = (bf16[4,8,8,128]{3,2,1,0:T(8,128)(2,1)S(1)}, bf16[4,8,8,128]{3,2,1,0:T(8,128)(2,1)S(1)}, u32[]{:S(2)}, u32[]{:S(2)}) collective-permute-start(bf16[4,8,8,128]{3,2,1,0:T(8,128)(2,1)S(1)} %bitcast.227), channel_id=1, source_target_pairs={{16,0},{17,1},{18,2},{19,3},{20,4},{21,5},{22,6},{23,7},{24,8},{25... | collective-permute-start | bytes 196616 | tf_op jit(solution)/shard_map/while/body/eval_jaxpr/ppermute | solution.py:28
  58.5 5.1 %collective-permute-start = (bf16[1,8,8,128]{3,2,1,0:T(8,128)(2,1)S(1)}, bf16[1,8,8,128]{3,2,1,0:T(8,128)(2,1)S(1)}, u32[]{:S(2)}, u32[]{:S(2)}) collective-permute-start(bf16[1,8,8,128]{3,2,1,0:T(8,128)(2,1)S(1)} %get-tuple-element.462), channel_id=1, source_target_pairs={{1,0},{2,1},{3,2},{4,3},{5,4},{6,5},{7,6},{8,7},{9,8},{10,9},{11,1... | collective-permute-start | bytes 49160 | tf_op jit(solution)/shard_map/while/body/eval_jaxpr/ppermute | solution.py:18
  59.8 4.5 %collective-permute-start.1 = (bf16[1,8,8,128]{3,2,1,0:T(8,128)(2,1)S(1)}, bf16[1,8,8,128]{3,2,1,0:T(8,128)(2,1)S(1)}, u32[]{:S(2)}, u32[]{:S(2)}) collective-permute-start(bf16[1,8,8,128]{3,2,1,0:T(8,128)(2,1)S(1)} %get-tuple-element.463), channel_id=1, source_target_pairs={{0,1},{1,2},{2,3},{3,4},{4,5},{5,6},{6,7},{7,8},{8,9},{9,10},{10,1... | collective-permute-start | bytes 49160 | tf_op jit(solution)/shard_map/while/body/eval_jaxpr/ppermute | solution.py:16
  64.8 1.2 copy-start.3
  66.6 8.1 %collective-permute-start.2 = (bf16[1,8,8,128]{3,2,1,0:T(8,128)(2,1)S(1)}, bf16[1,8,8,128]{3,2,1,0:T(8,128)(2,1)S(1)}, u32[]{:S(2)}, u32[]{:S(2)}) collective-permute-start(bf16[1,8,8,128]{3,2,1,0:T(8,128)(2,1)S(1)} %get-tuple-element.491), channel_id=1, source_target_pairs={{1,0},{2,1},{3,2},{4,3},{5,4},{6,5},{7,6},{8,7},{9,8},{10,9},{11,1... | collective-permute-start | bytes 49160 | tf_op jit(solution)/shard_map/while/body/eval_jaxpr/ppermute | solution.py:18
  67.9 6.9 %collective-permute-start.3 = (bf16[1,8,8,128]{3,2,1,0:T(8,128)(2,1)S(1)}, bf16[1,8,8,128]{3,2,1,0:T(8,128)(2,1)S(1)}, u32[]{:S(2)}, u32[]{:S(2)}) collective-permute-start(bf16[1,8,8,128]{3,2,1,0:T(8,128)(2,1)S(1)} %get-tuple-element.492), channel_id=1, source_target_pairs={{0,1},{1,2},{2,3},{3,4},{4,5},{5,6},{6,7},{7,8},{8,9},{9,10},{10,1... | collective-permute-start | bytes 49160 | tf_op jit(solution)/shard_map/while/body/eval_jaxpr/ppermute | solution.py:16
  76.6 6.2 %collective-permute-start.4 = (bf16[4,8,8,128]{3,2,1,0:T(8,128)(2,1)S(1)}, bf16[4,8,8,128]{3,2,1,0:T(8,128)(2,1)S(1)}, u32[]{:S(2)}, u32[]{:S(2)}) collective-permute-start(bf16[4,8,8,128]{3,2,1,0:T(8,128)(2,1)S(1)} %bitcast.227), channel_id=1, source_target_pairs={{16,0},{17,1},{18,2},{19,3},{20,4},{21,5},{22,6},{23,7},{24,8},{25... | collective-permute-start | bytes 196616 | tf_op jit(solution)/shard_map/while/body/eval_jaxpr/ppermute | solution.py:28
  82.7 1.2 copy-start
  82.7 163.2 %copy-start.2 = (bf16[2,4,8,8,128]{4,3,2,1,0:T(8,128)(2,1)}, bf16[2,4,8,8,128]{4,3,2,1,0:T(8,128)(2,1)S(1)}, u32[]{:S(2)}) copy-start(bf16[2,4,8,8,128]{4,3,2,1,0:T(8,128)(2,1)S(1)} %get-tuple-element.231) | copy-start | bytes 393220
Sparse Core Ops, SparseCore 0:
  84.1 151.1 all-gather.2
